TPU v7x, 512 devices: a whole 4x8x8 slice. The times are simulated.
512 devices in a mesh: member: 4 (over y_hi), lat: 8 (over x, core), lon: 16 (over z, y_lo).
Axes of the slice: x: 4, y: 8 (y_hi: 4, y_lo: 2; y = y_hi * 2 + y_lo), z: 8, core: 2. Of those that a mesh axis runs over, the one named last changes fastest.
Arguments:
- inputs: bfloat16 [4, 96, 8, 16, 5760], P('member', None, 'lat', 'lon'), may hold values from -6 to 6
- weight: bfloat16 [9, 8064], replicated, may hold values from -0.21875 to 0.21875
- bias: float32 [84], replicated, may hold values from -3 to 3
- analysis: bfloat16 [84, 8, 16, 5760], P(None, 'lat', 'lon'), may hold values from -7 to 7
- field_weight: float32 [84], replicated, may hold values from 0.25 to 2.5
Outputs:
- grad_input: bfloat16 [4, 96, 8, 16, 5760], P('member', None, 'lat', 'lon')
- grad_weight: float32 [9, 8064], replicated
- grad_bias: float32 [84], replicated
All inputs are finite; a program needn't handle non-finite values.
Results may differ from a plain program's by a relative error of at most 0.0053.
Values may be sent and summed in bfloat16 or wider, within the bound.
A program may use at most 128 MiB of HBM per device.

v0:
```python
import jax
import jax.numpy as jnp
from jax import lax
from jax.sharding import PartitionSpec as P

LAT_DEV = 64


def with_halo(shard, sides, width, wrap):
    for axis, dim in sides:
        peers, length = (lax.axis_size(axis), shard.shape[dim])
        up = [(i, (i + 1) % peers) for i in range(peers if wrap else peers - 1)]
        down = [(j, i) for i, j in up]
        last = lax.slice_in_dim(shard, length - width, length, axis=dim)
        initial = lax.slice_in_dim(shard, 0, width, axis=dim)
        before = lax.ppermute(last, axis, up)
        after = lax.ppermute(initial, axis, down)
        shard = jnp.concatenate([before, shard, after], axis=dim)
    return shard


def kernel_slope(values):
    return values * lax.rsqrt(values * values + 1.0)


def extend(grid_field):
    lat_padded = with_halo(grid_field, (("lat", 1),), 1, False)
    return with_halo(lat_padded, (("lon", 2),), 1, True)


def local(inputs, weight, bias, analysis, field_weight):
    chan_count = inputs.shape[1]
    cell_count = inputs.shape[4]
    lat_count = LAT_DEV
    lon_count = cell_count // lat_count
    field_count = analysis.shape[0]
    grid_field = inputs[0, :, 0, 0].reshape(chan_count, lat_count, lon_count)
    target_grid = analysis[:, 0, 0].reshape(field_count, lat_count, lon_count)
    members = lax.axis_size("member")
    tap_weights = weight.reshape(9, chan_count, field_count)
    padded = extend(grid_field)
    summed_terms = jnp.zeros((field_count, cell_count), jnp.float32)
    windows = []
    for tap_index in range(9):
        row_off = tap_index // 3
        col_off = tap_index % 3
        window = padded[:, row_off : row_off + lat_count, col_off : col_off + lon_count].reshape(
            chan_count, cell_count
        )
        windows.append(window)
        summed_terms = summed_terms + jnp.dot(
            tap_weights[tap_index].T, window, preferred_element_type=jnp.float32
        )
    summed_terms = summed_terms + bias[:, None]
    prediction = summed_terms.astype(jnp.bfloat16).reshape(field_count, lat_count, lon_count)
    scale_field = field_weight[:, None, None]
    quarter_rows = lat_count // members
    by_cells = lax.all_to_all(prediction[None], "member", split_axis=2, concat_axis=0, tiled=True)
    row_start = lax.axis_index("member") * quarter_rows
    target_rows = lax.dynamic_slice_in_dim(target_grid, row_start, quarter_rows, 1).astype(
        jnp.float32
    )
    member_values = by_cells.astype(jnp.float32)
    pair_slope = jnp.sum(kernel_slope(member_values[:, None] - member_values[None, :]), axis=1)
    target_slope = kernel_slope(member_values - target_rows[None])
    cell_grad = (
        scale_field[None] * (target_slope / members - pair_slope / (members * (members - 1)))
    ).astype(jnp.bfloat16)
    returned = lax.all_to_all(cell_grad, "member", split_axis=0, concat_axis=2, tiled=True)
    pred_grad = returned[0]
    grad_padded = extend(pred_grad)
    grad_flat = pred_grad.reshape(field_count, cell_count)
    input_terms = jnp.zeros((chan_count, cell_count), jnp.float32)
    weight_terms = []
    for tap_index in range(9):
        row_off = tap_index // 3
        col_off = tap_index % 3
        weight_terms.append(
            lax.dot_general(
                windows[tap_index],
                grad_flat,
                (((1,), (1,)), ((), ())),
                preferred_element_type=jnp.float32,
            )
        )
        grad_window = grad_padded[
            :, 2 - row_off : 2 - row_off + lat_count, 2 - col_off : 2 - col_off + lon_count
        ].reshape(field_count, cell_count)
        input_terms = input_terms + jnp.dot(
            tap_weights[tap_index], grad_window, preferred_element_type=jnp.float32
        )
    bias_terms = jnp.sum(grad_flat.astype(jnp.float32), axis=1)
    weight_total, bias_total = lax.psum(
        (jnp.stack(weight_terms), bias_terms), ("member", "lat", "lon")
    )
    global_cells = cell_count * lax.axis_size("lat") * lax.axis_size("lon")
    grad_input = input_terms.astype(jnp.bfloat16).reshape(1, chan_count, 1, 1, cell_count)
    grad_weight = (weight_total / global_cells).reshape(9, chan_count * field_count)
    grad_bias = bias_total / global_cells
    return (grad_input, grad_weight, grad_bias)


def solution(mesh):
    placed = (P("member", None, "lat", "lon", None), P(), P(), P(None, "lat", "lon", None), P())
    return jax.shard_map(
        local,
        mesh=mesh,
        in_specs=placed,
        out_specs=(P("member", None, "lat", "lon", None), P(), P()),
        check_vma=False,
    )
```

profile of v0, /device:TPU:1, one launch (start us, length us, event | category | flops | bytes accessed | tf_op | source)
XLA Modules:
  0.0 478.7 jit_solution(11899000557891740814)
XLA Ops:
  7.2 6.7 %reshape_squeeze.10 = bf16[96,64,90]{2,1,0:T(8,128)(2,1)S(1)} reshape(bf16[1,96,1,1,5760]{4,1,3,2,0:T(8,128)(2,1)} %param.5) | data formatting | bytes 2211840 | tf_op jit(solution)/shard_map/reshape;squeeze | solution.py:37
  14.0 4.5 collective-permute-start
  18.5 5.5 %collective-permute-start.1 = (bf16[96,1,90]{2,1,0:T(2,128)(2,1)S(1)}, bf16[96,1,90]{2,1,0:T(2,128)(2,1)S(1)}, u32[]{:S(2)}, u32[]{:S(2)}) collective-permute-start(bf16[96,1,90]{2,1,0:T(2,128)(2,1)S(1)} %get-tuple-element.25), channel_id=1, source_target_pairs={{16,0},{32,16},{48,32},{64,48},{80,64},{96,80},{112,96},{17,1},{33... | collective-permute-start | bytes 51848 | tf_op jit(solution)/shard_map/ppermute | solution.py:17
  37.0 8.9 %collective-permute-start.3 = (bf16[96,66,1]{0,1,2:T(8,128)(2,1)S(1)}, bf16[96,66,1]{0,1,2:T(8,128)(2,1)S(1)}, u32[]{:S(2)}, u32[]{:S(2)}) collective-permute-start(bf16[96,66,1]{0,1,2:T(8,128)(2,1)S(1)} %copy.45), channel_id=1, source_target_pairs={{1,0},{2,1},{3,2},{4,3},{5,4},{6,5},{7,6},{8,7},{9,8},{10,9},{11,1... | collective-permute-start | bytes 38024 | tf_op jit(solution)/shard_map/ppermute | solution.py:17
  48.9 4.3 reshape.96
  60.4 4.8 %pad_maximum_fusion.1 = (bf16[96,66,91]{2,1,0:T(8,128)(2,1)S(1)}, bf16[96,66,91]{2,1,0:T(8,128)(2,1)S(1)}) fusion(bf16[96,66,1]{2,1,0:T(8,128)(2,1)} %copy.46, bf16[96,1,90]{2,1,0:T(2,128)(2,1)S(1)} %collective-permute-done.1, bf16[96,64,90]{2,1,0:T(8,128)(2,1)S(1)} %reshape_squeeze.10, bf16[96,1,90]{2,1,0:T(2,128)(2,1)S(1)} %collective-permute-done, ...), kind=kLoop, calls=%fused_computation.35 | loop fusion | flops 9225216 | bytes 3472128 | tf_op jit(solution)/shard_map/concatenate | solution.py:18
  65.2 4.2 fusion.24
  69.4 4.1 reshape.95
  73.5 4.1 reshape.97
  87.4 4.5 reshape.102
  101.5 5.0 %broadcast_in_dim_reshape.3 = bf16[1,84,64,90]{3,2,1,0:T(8,128)(2,1)S(1)} reshape(bf16[84,5760]{1,0:T(8,128)(2,1)S(1)} %fusion.11) | data formatting | bytes 1935360 | tf_op jit(solution)/shard_map/broadcast_in_dim;reshape | solution.py:58
  108.6 5.9 %all-to-all-start = ((bf16[1,84,64,90]{3,1,0,2:T(8,128)(2,1)}), bf16[1,84,64,90]{3,1,0,2:T(8,128)(2,1)S(1)}, u32[]{:S(2)}, u32[]{:S(2)}) async-start(bf16[1,84,64,90]{3,1,0,2:T(8,128)(2,1)} %copy.47), calls=%async_computation | async-start | bytes 2883584 | tf_op jit(solution)/shard_map/all_to_all | solution.py:58
  114.5 7.0 %reshape_squeeze.11 = bf16[84,64,90]{2,1,0:T(8,128)(2,1)} reshape(bf16[84,1,1,5760]{3,0,2,1:T(8,128)(2,1)} %param.8) | data formatting | bytes 1935360 | tf_op jit(solution)/shard_map/reshape;squeeze | solution.py:38
  122.5 21.3 %all-to-all-done = bf16[1,84,64,90]{3,1,0,2:T(8,128)(2,1)S(1)} async-done(((bf16[1,84,64,90]{3,1,0,2:T(8,128)(2,1)}), bf16[1,84,64,90]{3,1,0,2:T(8,128)(2,1)S(1)}, u32[]{:S(2)}, u32[]{:S(2)}) %all-to-all-start) | async-done | bytes 967712 | tf_op jit(solution)/shard_map/all_to_all | solution.py:58
  148.1 33.6 %all_to_all.24 = bf16[4,84,16,90]{3,2,1,0:T(8,128)(2,1)S(1)} all-to-all(bf16[4,84,16,90]{3,2,1,0:T(8,128)(2,1)S(1)} %multiply_convert_fusion), channel_id=1, replica_groups=mesh['member'=4,'lat'=8,'lon'=16] {'member'}, dimensions={0} | all-to-all | bytes 1935360 | tf_op jit(solution)/shard_map/all_to_all | solution.py:69
  196.9 6.4 %collective-permute-start.4 = (bf16[84,1,90]{2,1,0:T(2,128)(2,1)S(1)}, bf16[84,1,90]{2,1,0:T(2,128)(2,1)S(1)}, u32[]{:S(2)}, u32[]{:S(2)}) collective-permute-start(bf16[84,1,90]{2,1,0:T(2,128)(2,1)S(1)} %get-tuple-element.40), channel_id=1, source_target_pairs={{0,16},{16,32},{32,48},{48,64},{64,80},{80,96},{96,112},{1,17},{17... | collective-permute-start | bytes 45368 | tf_op jit(solution)/shard_map/ppermute | solution.py:16
  207.3 101.3 %psum.15 = f32[84]{0:T(128)S(1)} all-reduce(f32[84]{0:T(128)S(1)} %convert_reduce_fusion), channel_id=1, replica_groups=mesh['member'=4,'lat'=8,'lon'=16] {'member','lat','lon'}, use_global_device_ids=true, to_apply=%region_3.0 | all-reduce | flops 84 | bytes 672 | tf_op jit(solution)/shard_map/psum | solution.py:93
  328.7 3.7 reshape.109
  337.7 5.2 %pad_maximum_fusion.5 = (bf16[84,66,91]{2,1,0:T(8,128)(2,1)S(1)}, bf16[84,66,91]{2,1,0:T(8,128)(2,1)}) fusion(bf16[84,66,1]{2,1,0:T(8,128)(2,1)} %copy.52, bf16[84,1,90]{2,1,0:T(2,128)(2,1)S(1)} %collective-permute-done.5, bf16[84,64,90]{2,1,0:T(8,128)(2,1)S(1)} %bitcast.145, bf16[84,1,90]{2,1,0:T(2,128)(2,1)S(1)} %collective-permute-done.4, ...), kind=kLoop, calls=%fused_computation.39 | loop fusion | flops 8072064 | bytes 3038112 | tf_op jit(solution)/shard_map/concatenate | solution.py:18
  345.9 3.7 reshape.103
  355.3 3.7 reshape.105
  359.0 3.9 reshape.106
  372.6 3.7 reshape.108
  384.8 84.4 %all-reduce.2.cloned.1.call-done = f32[9,96,84]{1,2,0:T(8,128)} async-done(((f32[9,96,84]{1,2,0:T(8,128)}), f32[9,96,84]{1,2,0:T(8,128)}) %all-reduce.2.cloned.1.call-update) | async-done | bytes 290320 | tf_op jit(solution)/shard_map/psum | solution.py:93
  (169 shorter events, 123.4 us)
Async XLA Ops:
  7.2 16.9 %copy-start.23 = (bf16[9,8064]{1,0:T(8,128)(2,1)S(1)}, bf16[9,8064]{1,0:T(8,128)(2,1)}, u32[]{:S(2)}) copy-start(bf16[9,8064]{1,0:T(8,128)(2,1)} %param.6) | copy-start | bytes 435460
  14.0 12.7 %collective-permute-start = (bf16[96,1,90]{2,1,0:T(2,128)(2,1)S(1)}, bf16[96,1,90]{2,1,0:T(2,128)(2,1)S(1)}, u32[]{:S(2)}, u32[]{:S(2)}) collective-permute-start(bf16[96,1,90]{2,1,0:T(2,128)(2,1)S(1)} %get-tuple-element.24), channel_id=1, source_target_pairs={{0,16},{16,32},{32,48},{48,64},{64,80},{80,96},{96,112},{1,17},{17... | collective-permute-start | bytes 51848 | tf_op jit(solution)/shard_map/ppermute | solution.py:16
  18.5 8.2 %collective-permute-start.1 = (bf16[96,1,90]{2,1,0:T(2,128)(2,1)S(1)}, bf16[96,1,90]{2,1,0:T(2,128)(2,1)S(1)}, u32[]{:S(2)}, u32[]{:S(2)}) collective-permute-start(bf16[96,1,90]{2,1,0:T(2,128)(2,1)S(1)} %get-tuple-element.25), channel_id=1, source_target_pairs={{16,0},{32,16},{48,32},{64,48},{80,64},{96,80},{112,96},{17,1},{33... | collective-permute-start | bytes 51848 | tf_op jit(solution)/shard_map/ppermute | solution.py:17
  24.9 66.9 %copy-start.36 = (bf16[96,84]{1,0:T(8,128)(2,1)}, bf16[96,84]{1,0:T(8,128)(2,1)S(1)}, u32[]{:S(2)}) copy-start(bf16[96,84]{1,0:T(8,128)(2,1)S(1)} %squeeze.39) | copy-start | bytes 48388
  25.1 69.5 %copy-start.34 = (bf16[96,84]{1,0:T(8,128)(2,1)}, bf16[96,84]{1,0:T(8,128)(2,1)S(1)}, u32[]{:S(2)}) copy-start(bf16[96,84]{1,0:T(8,128)(2,1)S(1)} %squeeze.40) | copy-start | bytes 48388
  25.2 70.6 %copy-start.30 = (bf16[96,84]{1,0:T(8,128)(2,1)}, bf16[96,84]{1,0:T(8,128)(2,1)S(1)}, u32[]{:S(2)}) copy-start(bf16[96,84]{1,0:T(8,128)(2,1)S(1)} %squeeze.41) | copy-start | bytes 48388
  25.4 71.7 %copy-start.28 = (bf16[96,84]{1,0:T(8,128)(2,1)}, bf16[96,84]{1,0:T(8,128)(2,1)S(1)}, u32[]{:S(2)}) copy-start(bf16[96,84]{1,0:T(8,128)(2,1)S(1)} %squeeze.42) | copy-start | bytes 48388
  25.7 68.4 %copy-start.24 = (bf16[96,84]{1,0:T(8,128)(2,1)}, bf16[96,84]{1,0:T(8,128)(2,1)S(1)}, u32[]{:S(2)}) copy-start(bf16[96,84]{1,0:T(8,128)(2,1)S(1)} %squeeze.44) | copy-start | bytes 48388
  25.8 72.5 %copy-start.32 = (bf16[96,84]{1,0:T(8,128)(2,1)}, bf16[96,84]{1,0:T(8,128)(2,1)S(1)}, u32[]{:S(2)}) copy-start(bf16[96,84]{1,0:T(8,128)(2,1)S(1)} %squeeze.43) | copy-start | bytes 48388
  32.5 23.9 %collective-permute-start.2 = (bf16[96,66,1]{0,1,2:T(8,128)(2,1)S(1)}, bf16[96,66,1]{0,1,2:T(8,128)(2,1)S(1)}, u32[]{:S(2)}, u32[]{:S(2)}) collective-permute-start(bf16[96,66,1]{0,1,2:T(8,128)(2,1)S(1)} %copy.43), channel_id=1, source_target_pairs={{0,1},{1,2},{2,3},{3,4},{4,5},{5,6},{6,7},{7,8},{8,9},{9,10},{10,1... | collective-permute-start | bytes 38024 | tf_op jit(solution)/shard_map/ppermute | solution.py:16
  37.0 21.5 %collective-permute-start.3 = (bf16[96,66,1]{0,1,2:T(8,128)(2,1)S(1)}, bf16[96,66,1]{0,1,2:T(8,128)(2,1)S(1)}, u32[]{:S(2)}, u32[]{:S(2)}) collective-permute-start(bf16[96,66,1]{0,1,2:T(8,128)(2,1)S(1)} %copy.45), channel_id=1, source_target_pairs={{1,0},{2,1},{3,2},{4,3},{5,4},{6,5},{7,6},{8,7},{9,8},{10,9},{11,1... | collective-permute-start | bytes 38024 | tf_op jit(solution)/shard_map/ppermute | solution.py:17
  83.7 9.9 %copy-start.4 = (bf16[96,5760]{1,0:T(8,128)(2,1)}, bf16[96,5760]{1,0:T(8,128)(2,1)S(1)}, u32[]{:S(2)}) copy-start(bf16[96,5760]{1,0:T(8,128)(2,1)S(1)} %reshape.100) | copy-start | bytes 3317764
  87.4 6.7 %copy-start.6 = (bf16[96,5760]{1,0:T(8,128)(2,1)}, bf16[96,5760]{1,0:T(8,128)(2,1)S(1)}, u32[]{:S(2)}) copy-start(bf16[96,5760]{1,0:T(8,128)(2,1)S(1)} %reshape.99) | copy-start | bytes 3317764
  108.6 35.3 %all-to-all-start = ((bf16[1,84,64,90]{3,1,0,2:T(8,128)(2,1)}), bf16[1,84,64,90]{3,1,0,2:T(8,128)(2,1)S(1)}, u32[]{:S(2)}, u32[]{:S(2)}) async-start(bf16[1,84,64,90]{3,1,0,2:T(8,128)(2,1)} %copy.47), calls=%async_computation | async-start | bytes 2883584 | tf_op jit(solution)/shard_map/all_to_all | solution.py:58
  114.5 354.8 %all-reduce.2.cloned.1.call-start = ((), (), s32[]{:S(2)}) async-start(), calls=%async_computation.2 | async-start | bytes 811008 | tf_op jit(solution)/shard_map/psum | solution.py:93
  185.5 3.6 copy-start.11
  196.9 112.2 %collective-permute-start.4 = (bf16[84,1,90]{2,1,0:T(2,128)(2,1)S(1)}, bf16[84,1,90]{2,1,0:T(2,128)(2,1)S(1)}, u32[]{:S(2)}, u32[]{:S(2)}) collective-permute-start(bf16[84,1,90]{2,1,0:T(2,128)(2,1)S(1)} %get-tuple-element.40), channel_id=1, source_target_pairs={{0,16},{16,32},{32,48},{48,64},{64,80},{80,96},{96,112},{1,17},{17... | collective-permute-start | bytes 45368 | tf_op jit(solution)/shard_map/ppermute | solution.py:16
  203.3 105.8 %collective-permute-start.5 = (bf16[84,1,90]{2,1,0:T(2,128)(2,1)S(1)}, bf16[84,1,90]{2,1,0:T(2,128)(2,1)S(1)}, u32[]{:S(2)}, u32[]{:S(2)}) collective-permute-start(bf16[84,1,90]{2,1,0:T(2,128)(2,1)S(1)} %get-tuple-element.41), channel_id=1, source_target_pairs={{16,0},{32,16},{48,32},{64,48},{80,64},{96,80},{112,96},{17,1},{33... | collective-permute-start | bytes 45368 | tf_op jit(solution)/shard_map/ppermute | solution.py:17
  314.8 17.6 %collective-permute-start.6 = (bf16[84,66,1]{0,1,2:T(8,128)(2,1)}, bf16[84,66,1]{0,1,2:T(8,128)(2,1)}, u32[]{:S(2)}, u32[]{:S(2)}) collective-permute-start(bf16[84,66,1]{0,1,2:T(8,128)(2,1)} %copy.51), channel_id=1, source_target_pairs={{1,0},{2,1},{3,2},{4,3},{5,4},{6,5},{7,6},{8,7},{9,8},{10,9},{11,1... | collective-permute-start | bytes 33272 | tf_op jit(solution)/shard_map/ppermute | solution.py:17
  320.7 14.3 %collective-permute-start.7 = (bf16[84,66,1]{0,1,2:T(8,128)(2,1)}, bf16[84,66,1]{0,1,2:T(8,128)(2,1)}, u32[]{:S(2)}, u32[]{:S(2)}) collective-permute-start(bf16[84,66,1]{0,1,2:T(8,128)(2,1)} %copy.53), channel_id=1, source_target_pairs={{0,1},{1,2},{2,3},{3,4},{4,5},{5,6},{6,7},{7,8},{8,9},{9,10},{10,1... | collective-permute-start | bytes 33272 | tf_op jit(solution)/shard_map/ppermute | solution.py:16
  345.9 3.7 copy-start.37
  349.6 3.2 copy-start
  359.0 3.9 copy-start.35
  372.6 3.7 copy-start.17
  (26 other events, 43.8 us)
Sparse Core Ops, SparseCore 0:
  196.9 272.2 all-reduce.1
where the time goes:
time: 487 us; the launch traced here: 479 us
  blocking collectives  135 us (28%)
  local copies, waits for them, and re-layouts  129 us (26%)
  waiting for transfers between devices  106 us (22%)
  starting transfers between devices  40.4 us (8%)
  matrix products  27.8 us (6%)
  other arithmetic  25.9 us (5%)
  between operations  14.9 us (3%)
    psum x1, blocking collectives, local(): lax.psum((jnp.stack(weight_terms), bias_terms), ('member', 'lat', 'lon'))  101 us
    psum x1, waiting for transfers between devices, local(): lax.psum((jnp.stack(weight_terms), bias_terms), ('member', 'lat', 'lon'))  84.4 us
    all_to_all x1, blocking collectives, local(): lax.all_to_all(cell_grad, 'member', split_axis=0, concat_axis=2, tiled=True)  33.6 us
    reshape x8, local copies, waits for them, and re-layouts, local(): padded[:, row_off:row_off + lat_count, col_off:col_off + lon_count]  29.9 us
    reshape x8, local copies, waits for them, and re-layouts, local(): grad_window = grad_padded[:, 2 - row_off:2 - row_off + lat_count, 2 - col...  28 us
    all_to_all x1, waiting for transfers between devices, local(): lax.all_to_all(prediction[None], 'member', split_axis=2, concat_axis=0, t...  21.3 us
    ppermute x4, starting transfers between devices, with_halo(): after = lax.ppermute(initial, axis, down)  19.4 us
    concatenate x6, other arithmetic, with_halo(): shard = jnp.concatenate([before, shard, after], axis=dim)  17.4 us
  transfers between devices with their start and end apart: 10, of which 2 were waited for; matrix products, arithmetic and copies ran while one was open for 20% of the time, Pallas kernels for 0%

commit v1 on v0

v1 whole, which is shorter than its diff:
```python
import numpy as np
import jax
import jax.numpy as jnp
from jax import lax
from jax.experimental import pallas as pl
from jax.experimental.pallas import tpu as pltpu
from jax.sharding import PartitionSpec as P

MESH = pl.DeviceIdType.MESH
C, F, ROWS, COLS = 96, 84, 64, 90
CELLS = ROWS * COLS
PITCH = COLS + 2
PAIRS = 24
CHUNKS = 6
STACK = 896
BF, F32 = jnp.bfloat16, jnp.float32
TAPS = [(a, b) for a in range(3) for b in range(3)]


def padded_source():
    lane = np.arange(PAIRS * 256)
    r, c = lane // PITCH, lane % PITCH
    inside = (r >= 1) & (r <= ROWS) & (c >= 1) & (c <= COLS)
    return np.where(inside, COLS * (r - 1) + c - 1, -1)


def dense_source():
    cell = np.arange(CELLS)
    return PITCH * (cell // COLS + 1) + cell % COLS + 1


def segments(source, tile):
    out = []
    for lane in range(128):
        src = source[tile * 128 + lane]
        key = (None, 0) if src < 0 else (int(src) // 128, int(lane - src) % 128)
        if not out or out[-1][1:] != key:
            out.append((lane,) + key)
    return out


def move_tile(source, tile, load, rows):
    lane = lax.broadcasted_iota(jnp.int32, (rows, 128), 1)
    acc = None
    for first, src, shift in segments(source, tile):
        if src is None:
            val = jnp.zeros((rows, 128), BF)
        else:
            val = load(src)
            if shift:
                val = pltpu.roll(val, shift, 1)
        acc = val if acc is None else jnp.where(lane >= first, val, acc)
    return acc


def lane_grid(p):
    o = p * 256 + lax.broadcasted_iota(jnp.int32, (1, 256), 1)
    r = lax.shift_right_logical(o * 45591, 22)
    c = o - r * PITCH
    return r, c


def interior(p):
    r, c = lane_grid(p)
    return (r >= 1) & (r <= ROWS) & (c >= 1) & (c <= COLS)


def slope(u):
    return u * lax.rsqrt(u * u + 1.0)


def edge_columns(grid):
    lane = lax.broadcasted_iota(jnp.int32, (C, 128), 1)
    first = last = jnp.zeros((C, 128), BF)
    for r in range(1, ROWS + 1):
        for col in (1, COLS):
            o = PITCH * r + col
            t, l = o // 128, o % 128
            val = grid[t // 2 + 1, t % 2]
            val = pltpu.roll(val, (r - l) % 128, 1)
            if col == 1:
                first = jnp.where(lane == r, val, first)
            else:
                last = jnp.where(lane == r, val, last)
    return first, last


def place_halo(grid, row_top, row_bottom, left, right, lat, n_lat):
    lane = lax.broadcasted_iota(jnp.int32, (C, 128), 1)
    zero = jnp.zeros((C, 128), BF)
    has_top = jnp.where(lat > 0, 1, 0)
    has_bottom = jnp.where(lat < n_lat - 1, 1, 0)
    top_on = jnp.broadcast_to(has_top, (C, 128)) == 1
    bottom_on = jnp.broadcast_to(has_bottom, (C, 128)) == 1

    def column(parts):
        above, own, below = parts
        val = jnp.where((lane >= 1) & (lane <= ROWS), own, zero)
        val = jnp.where((lane == 0) & top_on, pltpu.roll(above, 64, 1), val)
        return jnp.where((lane == ROWS + 1) & bottom_on, pltpu.roll(below, 64, 1), val)

    cl, cr = column(left), column(right)
    for t in range(2 * PAIRS):
        base = grid[t // 2 + 1, t % 2]
        if t == 0:
            base = jnp.where((lane >= 1) & (lane <= COLS), jnp.where(top_on, row_top[...], zero), base)
        if t == 46:
            base = jnp.where(lane >= 93, jnp.where(bottom_on, row_bottom[0], zero), base)
        if t == 47:
            base = jnp.where(lane <= 54, jnp.where(bottom_on, row_bottom[1], zero), base)
        for l in range(128):
            r, c = divmod(t * 128 + l, PITCH)
            if r > ROWS + 1:
                continue
            if c == 0:
                base = jnp.where(lane == l, pltpu.roll(cl, (l - r) % 128, 1), base)
            if c == PITCH - 1:
                base = jnp.where(lane == l, pltpu.roll(cr, (l - r) % 128, 1), base)
        grid[t // 2 + 1, t % 2] = base


def shifted(grid, p, sign):
    lane = lax.broadcasted_iota(jnp.int32, (C, 128), 1)
    tiles = (grid[p, 1], grid[p + 1, 0], grid[p + 1, 1], grid[p + 2, 0])
    wins = []
    for a, b in TAPS:
        d = sign * (PITCH * (a - 1) + b - 1)
        if d == 0:
            wins.append(jnp.concatenate([tiles[1], tiles[2]], axis=1))
            continue
        base, s = (0, d + 128) if d < 0 else (1, d)
        rolled = [pltpu.roll(tiles[base + i], 128 - s, 1) for i in range(3)]
        keep = lane < 128 - s
        wins.append(jnp.concatenate(
            [jnp.where(keep, rolled[0], rolled[1]), jnp.where(keep, rolled[1], rolled[2])], axis=1))
    return wins


def kernel(sizes, x_ref, wf_ref, wb_ref, bias_ref, an_ref, fw_ref, gi_ref, gw_ref,
           pg, gg, stack, pred, mv, sc, an_t, acc, gi_t,
           row_top, row_bottom, edge, side,
           grow_top, grow_bottom, gedge, gside,
           ar0, ar1, ar2, a1, a2, ar3, ar4, ar5,
           hs, hr, gs, gr, fs, fr, bs, br,
           s1, r1, s2, r2, s3, r3, s4, r4, s5, r5):
    n_mem, n_lat, n_lon = sizes
    n_z, n_y = n_lon // 2, n_mem * 2
    mem, lat, lon = (lax.axis_index(a) for a in ("member", "lat", "lon"))
    z, y_lo = lon // 2, lax.rem(lon, 2)
    y = mem * 2 + y_lo

    def wrap(v, n):
        return lax.rem(v + n, n)

    def at_y(t):
        return {"member": t // 2, "lon": z * 2 + lax.rem(t, 2)}

    def at_z(t):
        return {"lon": t * 2 + y_lo}

    zeros12 = jnp.zeros((2, C - F, 128), BF)
    for p in range(PAIRS + 2):
        gg[p, :, F:C, :] = zeros12
    for grid in (pg, gg):
        grid[0] = jnp.zeros((2, C, 128), BF)
        grid[PAIRS + 1] = jnp.zeros((2, C, 128), BF)

    barrier = pltpu.get_barrier_semaphore()

    def greet(dev):
        pl.semaphore_signal(barrier, inc=1, device_id=dev, device_id_type=MESH)

    for j in range(1, n_lat):
        greet({"lat": wrap(lat + j, n_lat)})
    for j in range(1, n_z):
        greet(at_z(wrap(z + j, n_z)))
    for j in range(1, n_y):
        greet(at_y(wrap(y + j, n_y)))
    for dl in (-1, 0, 1):
        for dn in (-1, 1):
            greet({"lat": wrap(lat + dl, n_lat), "lon": wrap(lon + dn, n_lon)})
    greetings = n_lat - 1 + n_z - 1 + n_y - 1 + 6

    source = padded_source()

    def load_x(t):
        return x_ref[:, 128 * t:128 * t + 128]

    for t in range(2 * PAIRS):
        pg[t // 2 + 1, t % 2] = move_tile(source, t, load_x, C)
    first, last = edge_columns(pg)
    edge[0] = first
    edge[1] = last

    pl.semaphore_wait(barrier, greetings)

    def halo_copies(grid, edges, top, bottom, sides, send, recv):
        copies = [
            pltpu.make_async_remote_copy(
                grid.at[1], bottom, send.at[0], recv.at[0],
                device_id={"lat": wrap(lat - 1, n_lat)}, device_id_type=MESH),
            pltpu.make_async_remote_copy(
                grid.at[PAIRS, 0], top, send.at[1], recv.at[1],
                device_id={"lat": wrap(lat + 1, n_lat)}, device_id_type=MESH)]
        for dl in (-1, 0, 1):
            for which, dn in ((0, -1), (1, 1)):
                i = 2 + (dl + 1) * 2 + which
                copies.append(pltpu.make_async_remote_copy(
                    edges.at[which], sides.at[which, dl + 1], send.at[i], recv.at[i],
                    device_id={"lat": wrap(lat - dl, n_lat), "lon": wrap(lon + dn, n_lon)},
                    device_id_type=MESH))
        return copies

    halo = halo_copies(pg, edge, row_top, row_bottom, side, hs, hr)
    for copy in halo:
        copy.start()

    def load_an(t):
        return an_ref[:, 128 * t:128 * t + 128]

    for t in range(2 * PAIRS):
        an_t[t // 2, t % 2] = move_tile(source, t, load_an, F)
    ones = jnp.ones((STACK - 9 * C, 256), BF)
    for p in range(PAIRS):
        stack[p, 9 * C:STACK, :] = ones
    acc[...] = jnp.zeros_like(acc)

    for copy in halo:
        copy.wait()
    place_halo(pg, row_top, row_bottom, [side[1, i] for i in range(3)],
               [side[0, i] for i in range(3)], lat, n_lat)

    def out_copy(k, j):
        dest = wrap(mem + j, n_mem)
        return pltpu.make_async_remote_copy(
            pred.at[k * 4 + dest], mv.at[k, j - 1], fs.at[k, j - 1], fr.at[k, j - 1],
            device_id={"member": dest}, device_id_type=MESH)

    def back_copy(k, j):
        dest = wrap(mem - j, n_mem)
        return pltpu.make_async_remote_copy(
            sc.at[k, j - 1], gg.at[k * 4 + mem + 1, :, 0:F, :], bs.at[k, j - 1], br.at[k, j - 1],
            device_id={"member": dest}, device_id_type=MESH)

    bias = bias_ref[...]

    def forward(k, carry):
        def one(w, inner):
            p = k * 4 + w
            for i, win in enumerate(shifted(pg, p, 1)):
                stack[p, C * i:C * i + C, :] = win
            out = jnp.dot(wf_ref[...], stack[p], preferred_element_type=F32) + bias
            out = out.astype(BF)
            pred[p, 0] = out[:, :128]
            pred[p, 1] = out[:, 128:]
            return inner
        lax.fori_loop(0, 4, one, 0)
        for j in (2, 1, 3):
            out_copy(k, j).start()
        return carry

    lax.fori_loop(0, CHUNKS, forward, 0)

    fw = fw_ref[...][None]

    def score(k, carry):
        own = k * 4 + mem
        for j in (1, 3, 2):
            out_copy(k, j).wait_recv()
        vals = [pred[own].astype(F32)] + [mv[k, j].astype(F32) for j in range(3)]
        target = an_t[own].astype(F32)
        pair = [None] * 4
        for i in range(4):
            for j in range(i + 1, 4):
                s = slope(vals[i] - vals[j])
                pair[i] = s if pair[i] is None else pair[i] + s
                pair[j] = -s if pair[j] is None else pair[j] - s
        for i in range(4):
            s = fw * (slope(vals[i] - target) * 0.25 - pair[i] / 12.0)
            if i == 0:
                gg[own + 1, :, 0:F, :] = s.astype(BF)
            else:
                sc[k, i - 1] = s.astype(BF)
        for j in (2, 1, 3):
            back_copy(k, j).start()
        return carry

    lax.fori_loop(0, CHUNKS, score, 0)

    def weight_pair(p):
        g = jnp.concatenate([gg[p + 1, 0], gg[p + 1, 1]], axis=1)
        g = jnp.where(jnp.broadcast_to(interior(p), (C, 256)), g, jnp.zeros_like(g))
        acc[...] += lax.dot_general(g, stack[p], (((1,), (1,)), ((), ())), preferred_element_type=F32)

    def weights(k, carry):
        weight_pair(k * 4 + mem)
        for j in (1, 3, 2):
            pltpu.make_async_remote_copy(
                sc.at[k, j - 1], gg.at[k * 4 + wrap(mem + j, n_mem) + 1, :, 0:F, :],
                bs.at[k, j - 1], br.at[k, j - 1],
                device_id={"member": wrap(mem - j, n_mem)}, device_id_type=MESH).wait_recv()
            weight_pair(k * 4 + wrap(mem + j, n_mem))
        return carry

    lax.fori_loop(0, CHUNKS, weights, 0)

    for q in range(80):
        i, j = divmod(q, 7)
        ar0[q // 10, q % 10] = acc[8 * i:8 * i + 8, 128 * j:128 * j + 128] if q < 77 else jnp.zeros((8, 128), F32)

    def windows(t):
        return (t * 8) // 7

    def phase1(j):
        dest = wrap(lat + j, n_lat)
        return pltpu.make_async_remote_copy(
            ar0.at[dest], ar1.at[j - 1], s1.at[j - 1], r1.at[j - 1],
            device_id={"lat": dest}, device_id_type=MESH)

    def phase2(j):
        dest = wrap(z + j, n_z)
        return pltpu.make_async_remote_copy(
            a1.at[pl.ds(windows(dest), 2)], ar2.at[j - 1], s2.at[j - 1], r2.at[j - 1],
            device_id=at_z(dest), device_id_type=MESH)

    def phase3(j, slot):
        return pltpu.make_async_remote_copy(
            a2, ar3.at[slot], s3.at[j - 1], r3.at[slot],
            device_id=at_y(wrap(y + j, n_y)), device_id_type=MESH)

    def phase4(j, slot):
        return pltpu.make_async_remote_copy(
            ar4.at[z], ar4.at[slot], s4.at[j - 1], r4.at[slot],
            device_id=at_z(wrap(z + j, n_z)), device_id_type=MESH)

    def phase5(j, slot):
        return pltpu.make_async_remote_copy(
            ar5.at[lat], ar5.at[slot], s5.at[j - 1], r5.at[slot],
            device_id={"lat": wrap(lat + j, n_lat)}, device_id_type=MESH)

    for j in range(1, n_lat):
        phase1(j).start()

    first, last = edge_columns(gg)
    gedge[0] = first
    gedge[1] = last
    ghalo = halo_copies(gg, gedge, grow_top, grow_bottom, gside, gs, gr)
    for copy in ghalo:
        copy.start()

    for j in range(1, n_lat):
        phase1(j).wait_recv()
    total = ar0[lat]
    for j in range(n_lat - 1):
        total = total + ar1[j]
    a1[...] = total
    for j in range(1, n_z):
        phase2(j).start()

    for copy in ghalo:
        copy.wait()
    place_halo(gg, grow_top, grow_bottom, [gside[1, i] for i in range(3)],
               [gside[0, i] for i in range(3)], lat, n_lat)

    def back(p, carry):
        rhs = jnp.concatenate(shifted(gg, p, -1), axis=0)
        out = jnp.dot(wb_ref[...], rhs, preferred_element_type=F32).astype(BF)
        gi_t[p, 0] = out[:, :128]
        gi_t[p, 1] = out[:, 128:]
        return carry

    lax.fori_loop(0, 8, back, 0)
    for j in range(1, n_z):
        phase2(j).wait_recv()
    total = a1[pl.ds(windows(z), 2)]
    for j in range(n_z - 1):
        total = total + ar2[j]
    a2[...] = total
    ar3[y] = total
    for j in range(1, n_y):
        phase3(j, y).start()

    lax.fori_loop(8, 16, back, 0)
    for j in range(1, n_y):
        phase3(j, wrap(y + j, n_y)).wait_recv()
    total = ar3[0]
    for j in range(1, n_y):
        total = total + ar3[j]
    ar4[z] = total
    for j in range(1, n_z):
        phase4(j, z).start()

    lax.fori_loop(16, 24, back, 0)
    for j in range(1, n_z):
        phase4(j, wrap(z + j, n_z)).wait_recv()
    for i in range(10):
        owner = max(t for t in range(8) if (t * 8) // 7 <= i)
        ar5[lat, i] = ar4[owner, i - (owner * 8) // 7]
    for j in range(1, n_lat):
        phase5(j, lat).start()

    dense = dense_source()

    def load_gi(t):
        return gi_t[t // 2, t % 2]

    for t in range(CELLS // 128):
        gi_ref[:, 128 * t:128 * t + 128] = move_tile(dense, t, load_gi, C)

    for j in range(1, n_lat):
        phase5(j, wrap(lat + j, n_lat)).wait_recv()
    for q in range(77):
        i, j = divmod(q, 7)
        gw_ref[8 * i:8 * i + 8, 128 * j:128 * j + 128] = ar5[q // 10, q % 10]

    def sent(k, carry):
        for j in (1, 2, 3):
            out_copy(k, j).wait_send()
            back_copy(k, j).wait_send()
        return carry

    lax.fori_loop(0, CHUNKS, sent, 0)
    for j in range(1, n_lat):
        phase1(j).wait_send()
        phase5(j, lat).wait_send()
    for j in range(1, n_z):
        phase2(j).wait_send()
        phase4(j, z).wait_send()
    for j in range(1, n_y):
        phase3(j, y).wait_send()


def solution(mesh):
    sizes = tuple(mesh.shape[a] for a in ("member", "lat", "lon"))

    def local(inputs, weight, bias, analysis, field_weight):
        x = inputs[0, :, 0, 0]
        target = analysis[:, 0, 0]
        taps = weight.reshape(9, C, F)
        wf = jnp.pad(taps.transpose(2, 0, 1).reshape(F, 9 * C), ((0, 0), (0, STACK - 9 * C)))
        wb = jnp.pad(taps, ((0, 0), (0, 0), (0, C - F))).transpose(1, 0, 2).reshape(C, 9 * C)
        vm = pltpu.VMEM
        dma = pltpu.SemaphoreType.DMA
        scratch = [
            vm((PAIRS + 2, 2, C, 128), BF),
            vm((PAIRS + 2, 2, C, 128), BF),
            vm((PAIRS, STACK, 256), BF),
            vm((PAIRS, 2, F, 128), BF),
            vm((CHUNKS, 3, 2, F, 128), BF),
            vm((CHUNKS, 3, 2, F, 128), BF),
            vm((PAIRS, 2, F, 128), BF),
            vm((C, STACK), F32),
            vm((PAIRS, 2, C, 128), BF),
            vm((C, 128), BF), vm((2, C, 128), BF), vm((2, C, 128), BF), vm((2, 3, C, 128), BF),
            vm((C, 128), BF), vm((2, C, 128), BF), vm((2, C, 128), BF), vm((2, 3, C, 128), BF),
            vm((8, 10, 8, 128), F32),
            vm((7, 10, 8, 128), F32),
            vm((7, 2, 8, 128), F32),
            vm((10, 8, 128), F32),
            vm((2, 8, 128), F32),
            vm((8, 2, 8, 128), F32),
            vm((8, 2, 8, 128), F32),
            vm((8, 10, 8, 128), F32),
            dma((8,)), dma((8,)), dma((8,)), dma((8,)),
            dma((CHUNKS, 3)), dma((CHUNKS, 3)), dma((CHUNKS, 3)), dma((CHUNKS, 3)),
            dma((7,)), dma((7,)), dma((7,)), dma((7,)), dma((7,)), dma((8,)),
            dma((7,)), dma((8,)), dma((7,)), dma((8,)),
        ]

        def body(*refs):
            kernel(sizes, *refs)

        gi, gw = pl.pallas_call(
            body,
            out_shape=(jax.ShapeDtypeStruct((C, CELLS), BF), jax.ShapeDtypeStruct((88, STACK), F32)),
            in_specs=[pl.BlockSpec(memory_space=vm)] * 6,
            out_specs=[pl.BlockSpec(memory_space=vm)] * 2,
            scratch_shapes=scratch,
            compiler_params=pltpu.CompilerParams(
                collective_id=0, has_side_effects=True, vmem_limit_bytes=56 * 2**20),
        )(x, wf, wb, bias[:, None], target, field_weight[:, None])
        cells = CELLS * sizes[1] * sizes[2]
        gw = gw[:F] / cells
        grad_weight = gw[:, :9 * C].reshape(F, 9, C).transpose(1, 2, 0).reshape(9, C * F)
        return gi.reshape(1, C, 1, 1, CELLS), grad_weight, gw[:, 9 * C]

    placed = (P("member", None, "lat", "lon", None), P(), P(), P(None, "lat", "lon", None), P())
    return jax.shard_map(
        local,
        mesh=mesh,
        in_specs=placed,
        out_specs=(P("member", None, "lat", "lon", None), P(), P()),
        check_vma=False,
    )
```

time: 487 us -> 122 us (0.25); the launches traced: 479 us -> 122 us
  blocking collectives: 135 us -> 0 us
  local copies, waits for them, and re-layouts: 129 us -> 9.4 us
  Pallas kernels: 0 us -> 111 us
  waiting for transfers between devices: 106 us -> 0 us
  starting transfers between devices: 40.4 us -> 0 us
  matrix products: 27.8 us -> 0 us
  other arithmetic: 25.9 us -> 1.09 us
  between operations: 14.9 us -> 0.67 us
    pallas_call x0 -> x1, Pallas kernels: none -> 111 us  [local(): pl.pallas_call(body, out_shape=(jax.ShapeDtypeStruct((C, CELLS), BF), jax...]
    psum x1 -> x0, blocking collectives: 101 us -> none  [local(): lax.psum((jnp.stack(weight_terms), bias_terms), ('member', 'lat', 'lon'))]
    psum x1 -> x0, waiting for transfers between devices: 84.4 us -> none  [local(): lax.psum((jnp.stack(weight_terms), bias_terms), ('member', 'lat', 'lon'))]
    reshape x17 -> x4, local copies, waits for them, and re-layouts: 59.1 us -> 3.85 us  [the longest x1 1.68 us: local(): taps = weight.reshape(9, C, F)]
    ppermute x8 -> x0, starting transfers between devices: 34.4 us -> none  [the longest x4 19.4 us: with_halo(): after = lax.ppermute(initial, axis, down)]
    all_to_all x1 -> x0, blocking collectives: 33.6 us -> none  [local(): lax.all_to_all(cell_grad, 'member', split_axis=0, concat_axis=2, tiled=True)]
    dot_general x27 -> x0, matrix products: 27.8 us -> none  [the longest x9 11.2 us: local(): lax.dot_general(windows[tap_index], grad_flat, (((1,), (1,)), ((), ())),...]
    slice x12 -> x2, local copies, waits for them, and re-layouts: 26 us -> 0.89 us  [the longest x1 0.69 us: local(): return (gi.reshape(1, C, 1, 1, CELLS), grad_weight, gw[:, 9 * C])]
  transfers between devices with their start and end apart: 10 -> 0, of which waited for: 2 -> 0; matrix products, arithmetic and copies ran while one was open for 20% -> 0% of each run, Pallas kernels for 0% -> 0%
where the time goes in v1:
time: 122 us
  Pallas kernels  111 us (91%)
  local copies, waits for them, and re-layouts  9.4 us (8%)
    pallas_call x1, Pallas kernels, local(): pl.pallas_call(body, out_shape=(jax.ShapeDtypeStruct((C, CELLS), BF), jax...  111 us

profile of v1, /device:TPU:1, one launch (start us, length us, event | category | flops | bytes accessed | tf_op | source)
XLA Modules:
  0.0 121.7 jit_solution(15887317303154043293)
XLA Ops:
  0.6 1.4 %copy.16.refs_3_ = f32[84,1]{1,0:T(8,128)} copy(f32[84,1]{0,1:T(1,128)} %bitcast.22) | data formatting | bytes 672 | tf_op jit(solution)/shard_map/broadcast_in_dim | solution.py:481
  2.0 1.4 %copy.17.refs_5_ = f32[84,1]{1,0:T(8,128)} copy(f32[84,1]{0,1:T(1,128)} %bitcast.23) | data formatting | bytes 672 | tf_op jit(solution)/shard_map/broadcast_in_dim | solution.py:481
  3.4 1.7 %reshape.24 = bf16[9,96,84]{2,1,0:T(8,128)(2,1)S(1)} reshape(bf16[9,8064]{1,0:T(8,128)(2,1)} %param.6) | data formatting | bytes 290304 | tf_op jit(solution)/shard_map/reshape | solution.py:439
  5.1 0.2 copy.13
  5.2 0.7 pad.8.refs_1_
  6.0 0.2 copy.14
  6.2 0.8 copy.15.refs_2_
  7.0 110.5 %shard_map.76 = (bf16[96,5760]{1,0:T(8,128)(2,1)}, f32[88,896]{1,0:T(8,128)}) custom-call(bf16[96,5760]{1,0:T(8,128)(2,1)} %bitcast.18, bf16[84,896]{1,0:T(8,128)(2,1)} %pad.8.refs_1_, bf16[96,864]{1,0:T(8,128)(2,1)} %copy.15.refs_2_, f32[84,1]{1,0:T(8,128)} %copy.16.refs_3_, bf16[84,5760]{1,0:T(8,128)(2,1)} %bitcast.20, f32[84,1]{1,0:T(8,128)} %copy.17.refs_5_), custom_call_target="tpu_custom_call" | custom-call | tf_op jit(solution)/shard_map/pallas_call | solution.py:473
  117.5 0.0 copy-start
  117.5 1.1 slice_multiply_fusion
  118.6 0.7 slice_reduce_fusion
  119.3 0.2 copy.18
  119.5 1.2 reshape.29
  120.7 0.0 copy-done
  120.7 1.0 copy.20
  (1 shorter events, 0.0 us)
Async XLA Ops:
  117.5 3.2 %copy-start = (bf16[96,5760]{1,0:T(8,128)(2,1)S(1)}, bf16[96,5760]{1,0:T(8,128)(2,1)}, u32[]{:S(2)}) copy-start(bf16[96,5760]{1,0:T(8,128)(2,1)} %get-tuple-element.5) | copy-start | bytes 3317764

commit v2 on v1

v2 whole, which is shorter than its diff:
```python
import numpy as np
import jax
import jax.numpy as jnp
from jax import lax
from jax.experimental import pallas as pl
from jax.experimental.pallas import tpu as pltpu
from jax.sharding import PartitionSpec as P

MESH = pl.DeviceIdType.MESH
C, F, ROWS, COLS = 96, 84, 64, 90
CELLS = ROWS * COLS
PITCH = COLS + 2
PAIRS = 24
CHUNKS = 6
STACK = 896
EARLY = 3
BACK = (3, 6, 9)
BF, F32 = jnp.bfloat16, jnp.float32
TAPS = [(a, b) for a in range(3) for b in range(3)]


def padded_source():
    lane = np.arange(PAIRS * 256)
    r, c = lane // PITCH, lane % PITCH
    inside = (r >= 1) & (r <= ROWS) & (c >= 1) & (c <= COLS)
    return np.where(inside, COLS * (r - 1) + c - 1, -1)


def dense_source():
    cell = np.arange(CELLS)
    return PITCH * (cell // COLS + 1) + cell % COLS + 1


def segments(source, tile):
    out = []
    for lane in range(128):
        src = source[tile * 128 + lane]
        key = (None, 0) if src < 0 else (int(src) // 128, int(lane - src) % 128)
        if not out or out[-1][1:] != key:
            out.append((lane,) + key)
    return out


def move_tile(source, tile, load, rows):
    lane = lax.broadcasted_iota(jnp.int32, (rows, 128), 1)
    acc = None
    for first, src, shift in segments(source, tile):
        if src is None:
            val = jnp.zeros((rows, 128), BF)
        else:
            val = load(src)
            if shift:
                val = pltpu.roll(val, shift, 1)
        acc = val if acc is None else jnp.where(lane >= first, val, acc)
    return acc


def lane_grid(p):
    o = p * 256 + lax.broadcasted_iota(jnp.int32, (1, 256), 1)
    r = lax.shift_right_logical(o * 45591, 22)
    c = o - r * PITCH
    return r, c


def interior(p):
    r, c = lane_grid(p)
    return (r >= 1) & (r <= ROWS) & (c >= 1) & (c <= COLS)


def slope(u):
    return u * lax.rsqrt(u * u + 1.0)


def edge_columns(grid, edges, rows):
    lane = lax.broadcasted_iota(jnp.int32, (C, 128), 1)
    found = [edges[0], edges[1]]
    for r in rows:
        for which, col in enumerate((1, COLS)):
            o = PITCH * r + col
            t, l = o // 128, o % 128
            val = grid[t // 2 + 1, t % 2]
            val = pltpu.roll(val, (r - l) % 128, 1)
            found[which] = jnp.where(lane == r, val, found[which])
    edges[0] = found[0]
    edges[1] = found[1]


def rows_of_chunk(k):
    return [r for r in range(1, ROWS + 1) if (PITCH * r + COLS) // (256 * 4) == k]


def place_halo(grid, arrived, lat, n_lat):
    lane = lax.broadcasted_iota(jnp.int32, (C, 128), 1)
    zero = jnp.zeros((C, 128), BF)
    has_top = jnp.where(lat > 0, 1, 0)
    has_bottom = jnp.where(lat < n_lat - 1, 1, 0)
    top_on = jnp.broadcast_to(has_top, (C, 128)) == 1
    bottom_on = jnp.broadcast_to(has_bottom, (C, 128)) == 1

    def column(at):
        above, own, below = (arrived[at + i] for i in range(3))
        val = jnp.where((lane >= 1) & (lane <= ROWS), own, zero)
        val = jnp.where((lane == 0) & top_on, pltpu.roll(above, 64, 1), val)
        return jnp.where((lane == ROWS + 1) & bottom_on, pltpu.roll(below, 64, 1), val)

    cl, cr = column(6), column(3)
    for t in range(2 * PAIRS):
        base = grid[t // 2 + 1, t % 2]
        if t == 0:
            base = jnp.where((lane >= 1) & (lane <= COLS), jnp.where(top_on, arrived[0], zero), base)
        if t == 46:
            base = jnp.where(lane >= 93, jnp.where(bottom_on, arrived[1], zero), base)
        if t == 47:
            base = jnp.where(lane <= 54, jnp.where(bottom_on, arrived[2], zero), base)
        for l in range(128):
            r, c = divmod(t * 128 + l, PITCH)
            if r > ROWS + 1:
                continue
            if c == 0:
                base = jnp.where(lane == l, pltpu.roll(cl, (l - r) % 128, 1), base)
            if c == PITCH - 1:
                base = jnp.where(lane == l, pltpu.roll(cr, (l - r) % 128, 1), base)
        grid[t // 2 + 1, t % 2] = base


def fill_stack(grid, p, sign, dst):
    lane = lax.broadcasted_iota(jnp.int32, (C, 128), 1)
    tiles = (grid[p, 1], grid[p + 1, 0], grid[p + 1, 1], grid[p + 2, 0], grid[p + 2, 1], grid[p + 3, 0])
    for i, (a, b) in enumerate(TAPS):
        d = sign * (PITCH * (a - 1) + b - 1)
        if d == 0:
            win = tiles[1:5]
        else:
            base, s = (0, d + 128) if d < 0 else (1, d)
            rolled = [pltpu.roll(tiles[base + n], 128 - s, 1) for n in range(5)]
            keep = lane < 128 - s
            win = [jnp.where(keep, rolled[n], rolled[n + 1]) for n in range(4)]
        for n in range(4):
            dst(n // 2)[C * i:C * i + C, 128 * (n % 2):128 * (n % 2) + 128] = win[n]


def kernel(sizes, x_hbm, an_hbm, w_hbm, bias_hbm, fw_hbm, gi_hbm, gw_ref, gb_ref,
           x_ref, an_ref, gi_ref, w_ref, bias_ref, fw_ref, wrows, picked, wf, wb, full,
           pg, gg, stack, bstack, pred, mv, sc, an_t, acc, gi_t,
           edge, arrived, gedge, garrived,
           ar0, ar1, ar2, a1, a2, ar3, ar4, ar5,
           pace, io, hs, hr, gs, gr, fs, fr, bs, br,
           s1, r1, s2, r2, s3, r3, s4, r4, s5, r5):
    n_mem, n_lat, n_lon = sizes
    n_z, n_y = n_lon // 2, n_mem * 2
    mem, lat, lon = (lax.axis_index(a) for a in ("member", "lat", "lon"))
    z, y_lo = lon // 2, lax.rem(lon, 2)
    y = mem * 2 + y_lo

    load_x = pltpu.make_async_copy(x_hbm, x_ref, io.at[0])
    load_an = pltpu.make_async_copy(an_hbm, an_ref, io.at[1])
    loads = [pltpu.make_async_copy(src, dst, io.at[3 + i]) for i, (src, dst) in enumerate(
        ((w_hbm, w_ref), (bias_hbm, bias_ref), (fw_hbm, fw_ref)))]
    load_x.start()
    for copy in loads:
        copy.start()
    load_an.start()

    def wrap(v, n):
        return lax.rem(v + n, n)

    def at_y(t):
        return {"member": t // 2, "lon": z * 2 + lax.rem(t, 2)}

    def at_z(t):
        return {"lon": t * 2 + y_lo}

    zeros12 = jnp.zeros((2, C - F, 128), BF)
    for p in range(PAIRS + 2):
        gg[p, :, F:C, :] = zeros12
    for p in (0, PAIRS + 1):
        gg[p, :, 0:F, :] = jnp.zeros((2, F, 128), BF)

    barrier = pltpu.get_barrier_semaphore()

    def greet(dev):
        pl.semaphore_signal(barrier, inc=1, device_id=dev, device_id_type=MESH)

    for dl in (-1, 0, 1):
        for dn in (-1, 1):
            greet({"lat": wrap(lat + dl, n_lat), "lon": wrap(lon + dn, n_lon)})
    for j in range(1, n_lat):
        greet({"lat": wrap(lat + j, n_lat)})
    for j in range(1, n_z):
        greet(at_z(wrap(z + j, n_z)))
    for j in range(1, n_y):
        greet(at_y(wrap(y + j, n_y)))
    greetings = n_lat - 1 + n_z - 1 + n_y - 1 + 6

    source = padded_source()
    for p in (0, PAIRS + 1):
        pg[p] = jnp.zeros((2, C, 128), BF)
    edge[...] = jnp.zeros_like(edge)
    load_x.wait()
    for t in range(2 * PAIRS):
        pg[t // 2 + 1, t % 2] = move_tile(source, t, lambda i: x_ref[:, 128 * i:128 * i + 128], C)
    edge_columns(pg, edge, range(1, ROWS + 1))

    pl.semaphore_wait(barrier, greetings)

    def landed(ref, sem):
        pltpu.make_async_copy(ref, ref, sem).wait()

    def halo_copies(grid, edges, into, send, recv):
        copies = []
        for dl in (-1, 1, 0):
            for which, dn in ((0, -1), (1, 1)):
                copies.append(pltpu.make_async_remote_copy(
                    edges.at[which], into.at[3 + 3 * which + dl + 1], send, recv,
                    device_id={"lat": wrap(lat - dl, n_lat), "lon": wrap(lon + dn, n_lon)},
                    device_id_type=MESH))
        copies += [
            pltpu.make_async_remote_copy(
                grid.at[1], into.at[1:3], send, recv,
                device_id={"lat": wrap(lat - 1, n_lat)}, device_id_type=MESH),
            pltpu.make_async_remote_copy(
                grid.at[PAIRS, 0], into.at[0], send, recv,
                device_id={"lat": wrap(lat + 1, n_lat)}, device_id_type=MESH)]
        return copies

    halo = halo_copies(pg, edge, arrived, hs, hr)
    for copy in halo:
        copy.start()

    for copy in loads:
        copy.wait()
    wf[:, 9 * C:STACK] = jnp.zeros((F, STACK - 9 * C), BF)
    wb[...] = jnp.zeros_like(wb)
    strips = C * F // 128
    for i in range(strips):
        wrows[16 * i:16 * i + 9, :] = w_ref[:, 128 * i:128 * i + 128].astype(F32)
    channel = lax.broadcasted_iota(jnp.int32, (C, strips), 0)
    strip = lax.broadcasted_iota(jnp.int32, (C, strips), 1)
    begin = lax.shift_right_logical(channel * F, 7)
    pick = jnp.concatenate(
        [jnp.where(strip == begin + n, 1.0, 0.0).astype(BF) for n in range(2)], axis=0)
    strip_rows = jnp.concatenate(
        [wrows[pl.ds(i, strips, stride=16), :].astype(BF) for i in range(9)], axis=1)
    picked[...] = jnp.dot(pick, strip_rows, preferred_element_type=F32)
    offset = (lax.broadcasted_iota(jnp.int32, (C, 128), 0) * F) & 127
    from_first = lax.broadcasted_iota(jnp.int32, (C, 128), 1) >= offset
    for i in range(9):
        tap = jnp.where(from_first, picked[0:C, 128 * i:128 * i + 128],
                        picked[C:2 * C, 128 * i:128 * i + 128])
        for bit in (4, 8, 16, 32, 64):
            tap = jnp.where((offset & bit) != 0, pltpu.roll(tap, 128 - bit, 1), tap)
        tap = tap[:, :F]
        wb[:, C * i:C * i + F] = tap.astype(BF)
        wf[:, C * i:C * i + C] = tap.T.astype(BF)

    def as_column(row):
        square = lax.broadcasted_iota(jnp.int32, (F, F), 0) == lax.broadcasted_iota(jnp.int32, (F, F), 1)
        return jnp.sum(jnp.where(square, jnp.broadcast_to(row, (F, F)), 0.0), axis=1, keepdims=True)

    bias = as_column(bias_ref[...])
    fw = as_column(fw_ref[...])[None]

    acc[...] = jnp.zeros_like(acc)
    gedge[...] = jnp.zeros_like(gedge)
    load_an.wait()
    for t in range(2 * PAIRS):
        an_t[t // 2, t % 2] = move_tile(source, t, lambda i: an_ref[:, 128 * i:128 * i + 128], F)
    ones = jnp.ones((STACK - 9 * C, 256), BF)
    for p in range(PAIRS):
        stack[p, 9 * C:STACK, :] = ones

    landed(arrived, hr)
    landed(arrived, hs)
    place_halo(pg, arrived, lat, n_lat)

    def out_copy(k, j):
        dest = wrap(mem + j, n_mem)
        return pltpu.make_async_remote_copy(
            pred.at[k * 4 + dest], mv.at[k, j - 1], fs.at[k, j - 1], fr.at[k, j - 1],
            device_id={"member": dest}, device_id_type=MESH)

    def back_copy(k, j):
        dest = wrap(mem - j, n_mem)
        return pltpu.make_async_remote_copy(
            sc.at[k, j - 1], gg.at[k * 4 + mem + 1, :, 0:F, :], bs.at[k, j - 1], br.at[k, j - 1],
            device_id={"member": dest}, device_id_type=MESH)

    def back_arrival(k, j):
        return pltpu.make_async_remote_copy(
            sc.at[k, j - 1], gg.at[k * 4 + wrap(mem + j, n_mem) + 1, :, 0:F, :],
            bs.at[k, j - 1], br.at[k, j - 1],
            device_id={"member": wrap(mem - j, n_mem)}, device_id_type=MESH)

    def forward(k):
        def one(h, inner):
            p = k * 4 + 2 * h
            fill_stack(pg, p, 1, lambda n: stack.at[p + n])
            for n in range(2):
                out = jnp.dot(wf[...], stack[p + n], preferred_element_type=F32) + bias
                out = out.astype(BF)
                pred[p + n, 0] = out[:, :128]
                pred[p + n, 1] = out[:, 128:]
            return inner
        lax.fori_loop(0, 2, one, 0)
        for j in (2, 1, 3):
            out_copy(k, j).start()

    def score(k):
        own = k * 4 + mem
        for j in (1, 3, 2):
            out_copy(k, j).wait_recv()
        vals = [pred[own].astype(F32)] + [mv[k, j].astype(F32) for j in range(3)]
        target = an_t[own].astype(F32)
        pair = [None] * 4
        for i in range(4):
            for j in range(i + 1, 4):
                s = slope(vals[i] - vals[j])
                pair[i] = s if pair[i] is None else pair[i] + s
                pair[j] = -s if pair[j] is None else pair[j] - s
        for i in (2, 1, 3, 0):
            s = fw * (slope(vals[i] - target) * 0.25 - pair[i] / 12.0)
            if i == 0:
                gg[own + 1, :, 0:F, :] = s.astype(BF)
            else:
                sc[k, i - 1] = s.astype(BF)

    def send_back(k):
        for j in (2, 1, 3):
            back_copy(k, j).start()

    def weight_pair(p):
        g = jnp.concatenate([gg[p + 1, 0], gg[p + 1, 1]], axis=1)
        g = jnp.where(jnp.broadcast_to(interior(p), (C, 256)), g, jnp.zeros_like(g))
        acc[...] += lax.dot_general(g, stack[p], (((1,), (1,)), ((), ())), preferred_element_type=F32)

    ghalo = halo_copies(gg, gedge, garrived, gs, gr)

    def weights(k):
        weight_pair(k * 4 + mem)
        for j in (1, 3):
            back_arrival(k, j).wait_recv()
            weight_pair(k * 4 + wrap(mem + j, n_mem))
        back_arrival(k, 2).wait_recv()
        for chunk in range(CHUNKS):
            @pl.when(k == chunk)
            def _():
                edge_columns(gg, gedge, rows_of_chunk(chunk))
                if chunk == CHUNKS - 1:
                    for copy in ghalo:
                        copy.start()
        weight_pair(k * 4 + wrap(mem + 2, n_mem))

    def each(first, last, step):
        def run(k, carry):
            step(k)
            return carry
        lax.fori_loop(first, last, run, 0)

    each(0, CHUNKS, forward)
    each(0, EARLY, score)
    other_lat = lat + 1 - 2 * lax.rem(lat, 2)
    other_lon = z * 2 + 1 - y_lo
    for dev in ({"lat": other_lat}, {"lon": other_lon}, {"lat": other_lat, "lon": other_lon}):
        pl.semaphore_signal(pace, inc=1, device_id=dev, device_id_type=MESH)
    pl.semaphore_wait(pace, 3)
    each(0, EARLY, send_back)

    def late(k):
        score(k)
        send_back(k)

    each(EARLY, CHUNKS, late)
    each(0, CHUNKS, weights)

    for q in range(80):
        i, j = divmod(q, 7)
        ar0[q // 10, q % 10] = acc[8 * i:8 * i + 8, 128 * j:128 * j + 128] if q < 77 else jnp.zeros((8, 128), F32)

    def windows(t):
        return (t * 8) // 7

    def phase1(j):
        dest = wrap(lat + j, n_lat)
        return pltpu.make_async_remote_copy(
            ar0.at[dest], ar1.at[j - 1], s1, r1,
            device_id={"lat": dest}, device_id_type=MESH)

    def phase2(j):
        dest = wrap(z + j, n_z)
        return pltpu.make_async_remote_copy(
            a1.at[pl.ds(windows(dest), 2)], ar2.at[j - 1], s2, r2,
            device_id=at_z(dest), device_id_type=MESH)

    def phase3(j, slot):
        return pltpu.make_async_remote_copy(
            a2, ar3.at[slot], s3, r3,
            device_id=at_y(wrap(y + j, n_y)), device_id_type=MESH)

    def phase4(j, slot):
        return pltpu.make_async_remote_copy(
            ar4.at[z], ar4.at[slot], s4, r4,
            device_id=at_z(wrap(z + j, n_z)), device_id_type=MESH)

    def phase5(j, slot):
        return pltpu.make_async_remote_copy(
            ar5.at[lat], ar5.at[slot], s5, r5,
            device_id={"lat": wrap(lat + j, n_lat)}, device_id_type=MESH)

    far_first = (4, 3, 5, 2, 6, 1, 7)
    for j in far_first:
        phase1(j).start()

    def back(h, carry):
        p = 2 * h
        fill_stack(gg, p, -1, lambda n: bstack.at[n])
        for n in range(2):
            out = jnp.dot(wb[...], bstack[n], preferred_element_type=F32).astype(BF)
            gi_t[p + n, 0] = out[:, :128]
            gi_t[p + n, 1] = out[:, 128:]
        return carry

    landed(ar1, r1)
    total = ar0[lat]
    for j in range(n_lat - 1):
        total = total + ar1[j]
    a1[...] = total
    for j in far_first:
        phase2(j).start()

    landed(garrived, gr)
    landed(garrived, gs)
    place_halo(gg, garrived, lat, n_lat)

    lax.fori_loop(0, BACK[0], back, 0)
    landed(ar2, r2)
    total = a1[pl.ds(windows(z), 2)]
    for j in range(n_z - 1):
        total = total + ar2[j]
    a2[...] = total
    ar3[y] = total
    for j in far_first:
        phase3(j, y).start()

    lax.fori_loop(BACK[0], BACK[1], back, 0)
    landed(ar3.at[0:7], r3)
    total = ar3[0]
    for j in range(1, n_y):
        total = total + ar3[j]
    ar4[z] = total
    for j in far_first:
        phase4(j, z).start()

    lax.fori_loop(BACK[1], BACK[2], back, 0)
    landed(ar4.at[0:7], r4)
    for i in range(10):
        owner = max(t for t in range(8) if (t * 8) // 7 <= i)
        ar5[lat, i] = ar4[owner, i - (owner * 8) // 7]
    for j in far_first:
        phase5(j, lat).start()

    lax.fori_loop(BACK[2], PAIRS // 2, back, 0)
    dense = dense_source()
    for t in range(CELLS // 128):
        gi_ref[:, 128 * t:128 * t + 128] = move_tile(dense, t, lambda i: gi_t[i // 2, i % 2], C)
    store_gi = pltpu.make_async_copy(gi_ref, gi_hbm, io.at[2])
    store_gi.start()

    def sent(k):
        for j in (1, 2, 3):
            out_copy(k, j).wait_send()
            back_copy(k, j).wait_send()

    each(0, CHUNKS, sent)
    landed(ar1, s1)
    landed(ar2, s2)
    landed(ar2, s3)
    landed(ar2, s4)
    landed(ar5.at[0:7], r5)
    scale = 1.0 / (CELLS * n_lat * n_lon)
    for q in range(77):
        i, j = divmod(q, 7)
        full[8 * i:8 * i + 8, 128 * j:128 * j + 128] = ar5[q // 10, q % 10] * scale
    for j in range(7):
        turned = full[:, 128 * j:128 * j + 128].T
        if j < 6:
            gw_ref[128 * j:128 * j + 128, :] = turned[:, :F]
        else:
            gw_ref[128 * j:9 * C, :] = turned[:9 * C - 128 * j, :F]
            gb_ref[...] = turned[9 * C - 128 * j:9 * C - 128 * j + 1, :F]
    landed(ar1, s5)
    store_gi.wait()


def solution(mesh):
    sizes = tuple(mesh.shape[a] for a in ("member", "lat", "lon"))

    def local(inputs, weight, bias, analysis, field_weight):
        x = inputs[0, :, 0, 0]
        target = analysis[:, 0, 0]
        vm = pltpu.VMEM
        dma = pltpu.SemaphoreType.DMA
        halo = [vm((2, C, 128), BF), vm((9, C, 128), BF)]
        scratch = [
            vm((C, CELLS), BF),
            vm((F, CELLS), BF),
            vm((C, CELLS), BF),
            vm((9, C * F), BF),
            vm((1, F), F32),
            vm((1, F), F32),
            vm((16 * (C * F // 128), 128), F32),
            vm((2 * C, 9 * 128), F32),
            vm((F, STACK), BF),
            vm((C, 9 * C), BF),
            vm((C, STACK), F32),
            vm((PAIRS + 2, 2, C, 128), BF),
            vm((PAIRS + 2, 2, C, 128), BF),
            vm((PAIRS, STACK, 256), BF),
            vm((2, 9 * C, 256), BF),
            vm((PAIRS, 2, F, 128), BF),
            vm((CHUNKS, 3, 2, F, 128), BF),
            vm((CHUNKS, 3, 2, F, 128), BF),
            vm((PAIRS, 2, F, 128), BF),
            vm((C, STACK), F32),
            vm((PAIRS, 2, C, 128), BF),
            *halo, *halo,
            vm((8, 10, 8, 128), F32),
            vm((7, 10, 8, 128), F32),
            vm((7, 2, 8, 128), F32),
            vm((10, 8, 128), F32),
            vm((2, 8, 128), F32),
            vm((8, 2, 8, 128), F32),
            vm((8, 2, 8, 128), F32),
            vm((8, 10, 8, 128), F32),
            pltpu.SemaphoreType.REGULAR,
            dma((6,)), dma, dma, dma, dma,
            *[dma((CHUNKS, 3))] * 4,
            *[dma] * 10,
        ]

        def body(*refs):
            kernel(sizes, *refs)

        here, far = pl.BlockSpec(memory_space=vm), pl.BlockSpec(memory_space=pl.ANY)
        gi, gw, gb = pl.pallas_call(
            body,
            out_shape=(jax.ShapeDtypeStruct((C, CELLS), BF), jax.ShapeDtypeStruct((9 * C, F), F32),
                       jax.ShapeDtypeStruct((1, F), F32)),
            in_specs=[far] * 5,
            out_specs=[far, here, here],
            scratch_shapes=scratch,
            compiler_params=pltpu.CompilerParams(
                collective_id=0, has_side_effects=True, vmem_limit_bytes=32 * 2**20),
        )(x, target, weight, bias[None], field_weight[None])
        return gi.reshape(1, C, 1, 1, CELLS), gw.reshape(9, C * F), gb[0]

    placed = (P("member", None, "lat", "lon", None), P(), P(), P(None, "lat", "lon", None), P())
    return jax.shard_map(
        local,
        mesh=mesh,
        in_specs=placed,
        out_specs=(P("member", None, "lat", "lon", None), P(), P()),
        check_vma=False,
    )
```

time: 122 us -> 108 us (0.89)
  Pallas kernels: 111 us -> 99.4 us
  local copies, waits for them, and re-layouts: 9.4 us -> 7.39 us
    pallas_call x1, Pallas kernels: 111 us -> 99.4 us  [local(): pl.pallas_call(body, out_shape=(jax.ShapeDtypeStruct((C, CELLS), BF), jax...]
    unnamed x3 -> x12, local copies, waits for them, and re-layouts: 0.99 us -> 6.21 us
    broadcast_in_dim x2 -> x0, local copies, waits for them, and re-layouts: 2.74 us -> none  [the longest x1 1.37 us: local(): bias[:, None]]
    reshape x4 -> x1, local copies, waits for them, and re-layouts: 3.85 us -> 1.18 us  [local(): return (gi.reshape(1, C, 1, 1, CELLS), gw.reshape(9, C * F), gb[0])]
where the time goes in v2:
time: 108 us; the launch traced here: 107 us
  Pallas kernels  99.4 us (92%)
  local copies, waits for them, and re-layouts  7.39 us (7%)
    pallas_call x1, Pallas kernels, local(): pl.pallas_call(body, out_shape=(jax.ShapeDtypeStruct((C, CELLS), BF), jax...  99.4 us
    unnamed x12, local copies, waits for them, and re-layouts  6.21 us

profile of v2, /device:TPU:1, one launch (start us, length us, event | category | flops | bytes accessed | tf_op | source)
XLA Modules:
  0.0 107.5 jit_solution(5358463788080478699)
XLA Ops:
  0.6 0.0 copy-start
  0.6 1.2 %copy-done = bf16[1,96,1,1,5760]{4,1,3,2,0:T(8,128)(2,1)S(1)} copy-done((bf16[1,96,1,1,5760]{4,1,3,2,0:T(8,128)(2,1)S(1)}, bf16[1,96,1,1,5760]{4,1,3,2,0:T(8,128)(2,1)}, u32[]{:S(2)}) %copy-start) | copy-done | bytes 1105944
  1.9 0.0 copy-start.1
  1.9 1.2 %copy-done.1 = bf16[84,1,1,5760]{3,0,2,1:T(8,128)(2,1)S(1)} copy-done((bf16[84,1,1,5760]{3,0,2,1:T(8,128)(2,1)S(1)}, bf16[84,1,1,5760]{3,0,2,1:T(8,128)(2,1)}, u32[]{:S(2)}) %copy-start.1) | copy-done | bytes 967704
  3.1 0.0 copy-start.2
  3.1 0.9 copy-done.2
  4.0 0.0 copy-start.3
  4.0 0.7 copy-done.3
  4.7 0.0 copy-start.4
  4.7 0.7 copy-done.4
  5.4 99.4 %shard_map.76 = (bf16[96,5760]{1,0:T(8,128)(2,1)S(1)}, f32[864,84]{1,0:T(8,128)S(1)}, f32[1,84]{1,0:T(1,128)S(1)}) custom-call(bf16[96,5760]{1,0:T(8,128)(2,1)S(1)} %bitcast.6, bf16[84,5760]{1,0:T(8,128)(2,1)S(1)} %bitcast.8, bf16[9,8064]{1,0:T(8,128)(2,1)S(1)} %copy-done.2, f32[1,84]{1,0:T(1,128)S(1)} %bitcast.9, f32[1,84]{1,0:T(1,128)S(1)} %bitcast.10), custom_call_target="tpu_custom_call" | custom-call | tf_op jit(solution)/shard_map/pallas_call | solution.py:544
  104.8 1.2 %reshape.13 = f32[9,8064]{1,0:T(8,128)} reshape(f32[864,84]{1,0:T(8,128)S(1)} %get-tuple-element.7) | data formatting | bytes 580608 | tf_op jit(solution)/shard_map/reshape | solution.py:554
  106.0 1.0 copy.10
  107.0 0.5 copy.11
Async XLA Ops:
  0.6 1.2 %copy-start = (bf16[1,96,1,1,5760]{4,1,3,2,0:T(8,128)(2,1)S(1)}, bf16[1,96,1,1,5760]{4,1,3,2,0:T(8,128)(2,1)}, u32[]{:S(2)}) copy-start(bf16[1,96,1,1,5760]{4,1,3,2,0:T(8,128)(2,1)} %param.5) | copy-start | bytes 3317764
  1.9 1.2 %copy-start.1 = (bf16[84,1,1,5760]{3,0,2,1:T(8,128)(2,1)S(1)}, bf16[84,1,1,5760]{3,0,2,1:T(8,128)(2,1)}, u32[]{:S(2)}) copy-start(bf16[84,1,1,5760]{3,0,2,1:T(8,128)(2,1)} %param.8) | copy-start | bytes 2903044
  3.1 0.9 copy-start.2
  4.0 0.7 copy-start.3
  4.7 0.7 copy-start.4

commit v3 on v2

--- a/solution.py
+++ b/solution.py
@@ -13,7 +13,7 @@
 PAIRS = 24
 CHUNKS = 6
 STACK = 896
-EARLY = 3
+EARLY = 2
 BACK = (3, 6, 9)
 BF, F32 = jnp.bfloat16, jnp.float32
 TAPS = [(a, b) for a in range(3) for b in range(3)]
@@ -89,7 +89,7 @@
     return [r for r in range(1, ROWS + 1) if (PITCH * r + COLS) // (256 * 4) == k]
 
 
-def place_halo(grid, arrived, lat, n_lat):
+def place_halo(grid, arrived, lat, n_lat, tiles=range(2 * PAIRS)):
     lane = lax.broadcasted_iota(jnp.int32, (C, 128), 1)
     zero = jnp.zeros((C, 128), BF)
     has_top = jnp.where(lat > 0, 1, 0)
@@ -104,7 +104,7 @@
         return jnp.where((lane == ROWS + 1) & bottom_on, pltpu.roll(below, 64, 1), val)
 
     cl, cr = column(6), column(3)
-    for t in range(2 * PAIRS):
+    for t in tiles:
         base = grid[t // 2 + 1, t % 2]
         if t == 0:
             base = jnp.where((lane >= 1) & (lane <= COLS), jnp.where(top_on, arrived[0], zero), base)
@@ -139,8 +139,8 @@
             dst(n // 2)[C * i:C * i + C, 128 * (n % 2):128 * (n % 2) + 128] = win[n]
 
 
-def kernel(sizes, x_hbm, an_hbm, w_hbm, bias_hbm, fw_hbm, gi_hbm, gw_ref, gb_ref,
-           x_ref, an_ref, gi_ref, w_ref, bias_ref, fw_ref, wrows, picked, wf, wb, full,
+def kernel(sizes, x_hbm, an_hbm, w_hbm, bias_hbm, fw_hbm, gi_hbm, gw_hbm, gb_hbm,
+           x_ref, an_ref, gi_ref, gw_ref, gb_ref, w_ref, bias_ref, fw_ref, wrows, picked, wf, wb, full,
            pg, gg, stack, bstack, pred, mv, sc, an_t, acc, gi_t,
            edge, arrived, gedge, garrived,
            ar0, ar1, ar2, a1, a2, ar3, ar4, ar5,
@@ -271,7 +271,7 @@
 
     landed(arrived, hr)
     landed(arrived, hs)
-    place_halo(pg, arrived, lat, n_lat)
+    place_halo(pg, arrived, lat, n_lat, range(10))
 
     def out_copy(k, j):
         dest = wrap(mem + j, n_mem)
@@ -356,7 +356,9 @@
             return carry
         lax.fori_loop(first, last, run, 0)
 
-    each(0, CHUNKS, forward)
+    each(0, 1, forward)
+    place_halo(pg, arrived, lat, n_lat, range(10, 2 * PAIRS))
+    each(1, CHUNKS, forward)
     each(0, EARLY, score)
     other_lat = lat + 1 - 2 * lax.rem(lat, 2)
     other_lon = z * 2 + 1 - y_lo
@@ -487,8 +489,13 @@
         else:
             gw_ref[128 * j:9 * C, :] = turned[:9 * C - 128 * j, :F]
             gb_ref[...] = turned[9 * C - 128 * j:9 * C - 128 * j + 1, :F]
+    stores = [store_gi, pltpu.make_async_copy(gw_ref, gw_hbm, io.at[6]),
+              pltpu.make_async_copy(gb_ref, gb_hbm, io.at[7])]
+    for copy in stores[1:]:
+        copy.start()
     landed(ar1, s5)
-    store_gi.wait()
+    for copy in stores:
+        copy.wait()
 
 
 def solution(mesh):
@@ -504,6 +511,8 @@
             vm((C, CELLS), BF),
             vm((F, CELLS), BF),
             vm((C, CELLS), BF),
+            vm((9 * C, F), F32),
+            vm((1, F), F32),
             vm((9, C * F), BF),
             vm((1, F), F32),
             vm((1, F), F32),
@@ -532,7 +541,7 @@
             vm((8, 2, 8, 128), F32),
             vm((8, 10, 8, 128), F32),
             pltpu.SemaphoreType.REGULAR,
-            dma((6,)), dma, dma, dma, dma,
+            dma((8,)), dma, dma, dma, dma,
             *[dma((CHUNKS, 3))] * 4,
             *[dma] * 10,
         ]
@@ -540,17 +549,17 @@
         def body(*refs):
             kernel(sizes, *refs)
 
-        here, far = pl.BlockSpec(memory_space=vm), pl.BlockSpec(memory_space=pl.ANY)
+        stay = pl.BlockSpec(memory_space=pltpu.HBM)
         gi, gw, gb = pl.pallas_call(
             body,
             out_shape=(jax.ShapeDtypeStruct((C, CELLS), BF), jax.ShapeDtypeStruct((9 * C, F), F32),
                        jax.ShapeDtypeStruct((1, F), F32)),
-            in_specs=[far] * 5,
-            out_specs=[far, here, here],
+            in_specs=[stay] * 5,
+            out_specs=[pl.BlockSpec(memory_space=pl.ANY)] * 3,
             scratch_shapes=scratch,
             compiler_params=pltpu.CompilerParams(
                 collective_id=0, has_side_effects=True, vmem_limit_bytes=32 * 2**20),
-        )(x, target, weight, bias[None], field_weight[None])
+        )(*(pltpu.with_memory_space_constraint(v, pltpu.HBM) for v in (x, target, weight, bias[None], field_weight[None])))
         return gi.reshape(1, C, 1, 1, CELLS), gw.reshape(9, C * F), gb[0]
 
     placed = (P("member", None, "lat", "lon", None), P(), P(), P(None, "lat", "lon", None), P())

time: 108 us -> 101 us (0.935)
  local copies, waits for them, and re-layouts: 7.39 us -> 2.68 us
  Pallas kernels: 99.4 us -> 97.4 us
    unnamed x12 -> x2, local copies, waits for them, and re-layouts: 6.21 us -> 1.5 us
    pallas_call x1, Pallas kernels: 99.4 us -> 97.4 us  [local(): pl.pallas_call(body, out_shape=(jax.ShapeDtypeStruct((C, CELLS), BF), jax...]
where the time goes in v3:
time: 101 us
  Pallas kernels  97.4 us (96%)
  local copies, waits for them, and re-layouts  2.68 us (3%)
    pallas_call x1, Pallas kernels, local(): pl.pallas_call(body, out_shape=(jax.ShapeDtypeStruct((C, CELLS), BF), jax...  97.4 us

profile of v3, /device:TPU:1, one launch (start us, length us, event | category | flops | bytes accessed | tf_op | source)
XLA Modules:
  0.0 100.8 jit_solution(16160236371585972881)
XLA Ops:
  0.6 97.4 %shard_map.76 = (bf16[96,5760]{1,0:T(8,128)(2,1)S(1)}, f32[864,84]{1,0:T(8,128)S(1)}, f32[1,84]{1,0:T(1,128)S(1)}) custom-call(bf16[96,5760]{1,0:T(8,128)(2,1)} %bitcast.8, bf16[84,5760]{1,0:T(8,128)(2,1)} %bitcast.9, bf16[9,8064]{1,0:T(8,128)(2,1)} %refs_2_.1, f32[1,84]{1,0:T(1,128)} %bitcast.10, f32[1,84]{1,0:T(1,128)} %bitcast.11), custom_call_target="tpu_custom_call" | custom-call | tf_op jit(solution)/shard_map/pallas_call | solution.py:553
  98.1 1.2 %reshape.13 = f32[9,8064]{1,0:T(8,128)} reshape(f32[864,84]{1,0:T(8,128)S(1)} %get-tuple-element.7) | data formatting | bytes 580608 | tf_op jit(solution)/shard_map/reshape | solution.py:563
  99.3 1.0 copy.10
  100.2 0.5 copy.11

commit v4 on v3

--- a/solution.py
+++ b/solution.py
@@ -13,7 +13,7 @@
 PAIRS = 24
 CHUNKS = 6
 STACK = 896
-EARLY = 2
+EARLY = 1
 BACK = (3, 6, 9)
 BF, F32 = jnp.bfloat16, jnp.float32
 TAPS = [(a, b) for a in range(3) for b in range(3)]
@@ -152,11 +152,15 @@
     z, y_lo = lon // 2, lax.rem(lon, 2)
     y = mem * 2 + y_lo
 
-    load_x = pltpu.make_async_copy(x_hbm, x_ref, io.at[0])
+    third = CELLS // 3
+    load_x = [pltpu.make_async_copy(
+        x_hbm.at[:, third * i:third * i + third], x_ref.at[:, third * i:third * i + third],
+        io.at[(0, 8, 9)[i]]) for i in range(3)]
     load_an = pltpu.make_async_copy(an_hbm, an_ref, io.at[1])
     loads = [pltpu.make_async_copy(src, dst, io.at[3 + i]) for i, (src, dst) in enumerate(
         ((w_hbm, w_ref), (bias_hbm, bias_ref), (fw_hbm, fw_ref)))]
-    load_x.start()
+    for copy in load_x:
+        copy.start()
     for copy in loads:
         copy.start()
     load_an.start()
@@ -196,8 +200,12 @@
     for p in (0, PAIRS + 1):
         pg[p] = jnp.zeros((2, C, 128), BF)
     edge[...] = jnp.zeros_like(edge)
-    load_x.wait()
+    load_x[0].wait()
+    here = 0
     for t in range(2 * PAIRS):
+        while here < 2 and source[128 * t:128 * t + 128].max() >= third * (here + 1):
+            here += 1
+            load_x[here].wait()
         pg[t // 2 + 1, t % 2] = move_tile(source, t, lambda i: x_ref[:, 128 * i:128 * i + 128], C)
     edge_columns(pg, edge, range(1, ROWS + 1))
 
@@ -541,7 +549,7 @@
             vm((8, 2, 8, 128), F32),
             vm((8, 10, 8, 128), F32),
             pltpu.SemaphoreType.REGULAR,
-            dma((8,)), dma, dma, dma, dma,
+            dma((10,)), dma, dma, dma, dma,
             *[dma((CHUNKS, 3))] * 4,
             *[dma] * 10,
         ]

time: 101 us -> 100 us (0.990)
  no operation moved by 1% of the time
where the time goes in v4:
time: 100 us
  Pallas kernels  97 us (97%)
  local copies, waits for them, and re-layouts  2.68 us (3%)
    pallas_call x1, Pallas kernels, local(): pl.pallas_call(body, out_shape=(jax.ShapeDtypeStruct((C, CELLS), BF), jax...  97 us

profile of v4, /device:TPU:1, one launch (start us, length us, event | category | flops | bytes accessed | tf_op | source)
XLA Modules:
  0.0 100.3 jit_solution(11355911884975949111)
XLA Ops:
  0.6 97.0 %shard_map.76 = (bf16[96,5760]{1,0:T(8,128)(2,1)S(1)}, f32[864,84]{1,0:T(8,128)S(1)}, f32[1,84]{1,0:T(1,128)S(1)}) custom-call(bf16[96,5760]{1,0:T(8,128)(2,1)} %bitcast.8, bf16[84,5760]{1,0:T(8,128)(2,1)} %bitcast.9, bf16[9,8064]{1,0:T(8,128)(2,1)} %refs_2_.1, f32[1,84]{1,0:T(1,128)} %bitcast.10, f32[1,84]{1,0:T(1,128)} %bitcast.11), custom_call_target="tpu_custom_call" | custom-call | tf_op jit(solution)/shard_map/pallas_call | solution.py:561
  97.6 1.2 %reshape.13 = f32[9,8064]{1,0:T(8,128)} reshape(f32[864,84]{1,0:T(8,128)S(1)} %get-tuple-element.7) | data formatting | bytes 580608 | tf_op jit(solution)/shard_map/reshape | solution.py:571
  98.8 1.0 copy.10
  99.8 0.5 copy.11
